TPU v7x, 32 devices: a whole 2x2x4 slice. The times are simulated.
32 devices in a mesh: blk: 4 (over z), virt: 8 (over y, x, core).
Axes of the slice: x: 2, y: 2, z: 4, core: 2. Of those that a mesh axis runs over, the one named last changes fastest.
Arguments:
- integrals: bfloat16 [512, 16, 4096], P(('blk', 'virt')), may hold values from -0.09375 to 0.09375
- amplitudes: bfloat16 [256, 4096], P('blk'), may hold values from -6 to 6
- readers: int32 [512], P(('blk', 'virt')), may hold values from 0 to 7, as said below
- row_slots: int32 [512], P(('blk', 'virt')), may hold values from 0 to 3
- tile_mask: int32 [512, 4], P(('blk', 'virt')), may hold values 0 or 1
- virt_energy: float32 [2048], P(('blk', 'virt')), may hold values from 1 to 3
- occ_energy: float32 [1200], replicated, may hold values from -1 to -0.25
- pair_first: int32 [256], replicated, may hold values from 0 to 1199
- pair_second: int32 [256], replicated, may hold values from 0 to 1199
Outputs:
- update: bfloat16 [2048, 256], P(('blk', 'virt'))
Inputs may be any that keep to these rules, and one draw needn't show every extreme that they name: `readers`: each tile names a reader on the virt axis in the same blk row as its generating device; one device names one reader at most 4 times, and in every blk row some reader is named 4 times by every device of that row.
All inputs are finite; a program needn't handle non-finite values. No bound on the sum of `tile_mask` on one device may be relied on, other than what follows from the above.
Results may differ from a plain program's by a relative error of at most 0.001.
Values may be sent and summed in bfloat16 or wider, within the bound.
A program may use at most 64 MiB of HBM per device.

v0:
```python
import jax
import jax.numpy as jnp
from jax import lax
from jax.sharding import PartitionSpec as P


def body(
    integrals,
    amplitudes,
    readers,
    row_slots,
    tile_mask,
    virt_energy,
    occ_energy,
    pair_first,
    pair_second,
):
    virt_count = lax.axis_size("virt")
    blk_count = lax.axis_size("blk")
    generated = integrals.shape[0]
    tile_rows = integrals.shape[1]
    panel_rows = amplitudes.shape[0]
    capacity = max(1, 2 * generated // virt_count)
    slot_count = virt_count * capacity
    row_blocks = virt_energy.shape[0] // tile_rows
    tile_order = jnp.arange(generated, dtype=jnp.int32)
    same_reader = readers[:, None] == readers[None, :]
    earlier = tile_order[None, :] < tile_order[:, None]
    within = jnp.sum((same_reader & earlier).astype(jnp.int32), axis=1)
    position = readers * capacity + within
    placing = jnp.arange(slot_count, dtype=jnp.int32)[:, None] == position[None, :]
    filled = jnp.any(placing, axis=1)
    source_tile = jnp.sum(placing.astype(jnp.int32) * tile_order[None, :], axis=1)
    row_hot = (row_slots[:, None] == jnp.arange(row_blocks, dtype=jnp.int32)[None, :]).astype(
        jnp.float32
    )
    mask_float = tile_mask.astype(jnp.float32)
    sent_tiles = jnp.where(
        filled[:, None, None], integrals[source_tile], jnp.zeros((), jnp.bfloat16)
    )
    coefficient = (row_hot[:, :, None] * mask_float[:, None, :]).reshape(
        generated, row_blocks * blk_count
    )
    sent_coef = jnp.where(filled[:, None], coefficient[source_tile], 0.0).astype(jnp.bfloat16)
    got_tiles, got_coef = (
        lax.all_to_all(sent_tiles, "virt", split_axis=0, concat_axis=0, tiled=True),
        lax.all_to_all(sent_coef, "virt", split_axis=0, concat_axis=0, tiled=True),
    )
    got_coef = got_coef.astype(jnp.float32).reshape(slot_count, row_blocks, blk_count)
    panel = lax.all_gather(amplitudes, "blk", axis=0, tiled=True)
    column_count = panel.shape[0]
    column_panel = jnp.arange(column_count, dtype=jnp.int32) // panel_rows
    columns = jnp.einsum(
        "srk,kp->srp",
        got_coef,
        (jnp.arange(blk_count, dtype=jnp.int32)[:, None] == column_panel[None, :]).astype(
            jnp.float32
        ),
        precision=lax.Precision.HIGHEST,
    )
    product = jnp.einsum("stw,pw->stp", got_tiles, panel, preferred_element_type=jnp.float32)
    summed_panel = jnp.einsum("srp,stp->rtp", columns, product, precision=lax.Precision.HIGHEST)
    summed = summed_panel.reshape(row_blocks * tile_rows, column_count)
    levels = jnp.arange(occ_energy.shape[0], dtype=jnp.int32)[None, :]
    first_energy = jnp.sum(
        jnp.where(pair_first[:, None] == levels, occ_energy[None, :], 0.0), axis=1
    )
    second_energy = jnp.sum(
        jnp.where(pair_second[:, None] == levels, occ_energy[None, :], 0.0), axis=1
    )
    denominator = virt_energy[:, None] - first_energy[None, :] - second_energy[None, :]
    return (summed / denominator).astype(jnp.bfloat16)


def solution(mesh):
    placed = (
        P(("blk", "virt"), None, None),
        P("blk", None),
        P(("blk", "virt")),
        P(("blk", "virt")),
        P(("blk", "virt"), None),
        P(("blk", "virt")),
        P(),
        P(),
        P(),
    )
    return jax.shard_map(
        body, mesh=mesh, in_specs=placed, out_specs=P(("blk", "virt"), None), check_vma=False
    )
```

profile of v0, /device:TPU:0, one launch (start us, length us, event | category | flops | bytes accessed | tf_op | source)
XLA Modules:
  0.0 97.9 jit_solution(15406979760878977125)
XLA Ops:
  6.5 1.0 %convert_reduce_fusion = s32[16]{0:T(128)S(1)} fusion(s32[16]{0:T(128)} %param.11), kind=kLoop, calls=%fused_computation.16 | loop fusion | flops 1264 | bytes 128 | tf_op jit(solution)/shard_map/reduce_sum | solution.py:29
  7.5 0.7 multiply_add_fusion
  8.2 0.1 select_reduce_fusion.2
  8.3 0.1 fusion.5
  8.4 0.7 convert_element_type.25
  9.1 0.7 fusion.10
  9.8 0.1 copy.20
  9.8 0.1 broadcast_in_dim.44
  9.9 0.6 gather_fusion.1
  10.5 0.7 select_convert_fusion
  11.2 5.2 %all-to-all-start.1 = ((bf16[8,4,16]{2,1,0:T(4,128)(2,1)}), bf16[8,4,16]{2,1,0:T(4,128)(2,1)S(1)}, u32[]{:S(2)}, u32[]{:S(2)}) async-start(bf16[8,4,16]{2,1,0:T(4,128)(2,1)} %select_convert_fusion), calls=%async_computation.1 | async-start | bytes 16384 | tf_op jit(solution)/shard_map/all_to_all | solution.py:47
  16.4 2.8 %gather_fusion = bf16[32,16,4096]{2,1,0:T(8,128)(2,1)} fusion(bf16[16,16,4096]{2,1,0:T(8,128)(2,1)S(1)} %copy-done, s32[1024]{0:T(1024)S(1)} %pad_clamp_fusion), kind=kCustom, calls=%fused_computation | custom fusion | bytes 8388736 | tf_op jit(solution)/shard_map/gather | solution.py:39
  19.2 4.5 %broadcast_select_fusion = bf16[32,16,4096]{2,1,0:T(8,128)(2,1)} fusion(bf16[32,16,4096]{2,1,0:T(8,128)(2,1)} %gather_fusion, pred[32]{0:T(512)(128)(4,1)S(1)} %fusion.5), kind=kLoop, calls=%fused_computation.2 | loop fusion | flops 2097152 | bytes 8388640 | tf_op jit(solution)/shard_map/jit(_where)/select_n | solution.py:38
  23.7 4.7 %all-to-all-start = ((bf16[32,16,4096]{2,1,0:T(8,128)(2,1)}), bf16[32,16,4096]{2,1,0:T(8,128)(2,1)}, u32[]{:S(2)}, u32[]{:S(2)}) async-start(bf16[32,16,4096]{2,1,0:T(8,128)(2,1)} %broadcast_select_fusion), calls=%async_computation | async-start | bytes 8388608 | tf_op jit(solution)/shard_map/all_to_all | solution.py:46
  28.4 0.7 all-gather.2.cloned.1.call-update
  29.2 0.4 select_reduce_fusion.1
  29.6 0.1 fusion.3
  29.8 0.2 copy.23
  30.0 48.4 %all-gather.2.cloned.1.call-done = bf16[256,4096]{1,0:T(8,128)(2,1)} async-done(((bf16[64,4096]{1,0:T(8,128)(2,1)}), bf16[256,4096]{1,0:T(8,128)(2,1)}) %all-gather.2.cloned.1.call-update) | async-done | bytes 2097168 | tf_op jit(solution)/shard_map/all_gather | solution.py:50
  78.4 4.1 %fusion = f32[32,16,256]{2,1,0:T(8,128)S(1)} fusion(bf16[32,16,4096]{2,1,0:T(8,128)(2,1)} %all-to-all-done, bf16[256,4096]{1,0:T(8,128)(2,1)} %all-gather.2.cloned.1.call-done), kind=kOutput, calls=%fused_computation.3 | convolution fusion | flops 1073741824 | bytes 6815744 | tf_op jit(solution)/shard_map/stw,pw->stp/dot_general | solution.py:61
  82.6 2.6 %copy.22 = f32[32,16,256]{0,1,2:T(8,128)} copy(f32[32,16,256]{2,1,0:T(8,128)S(1)} %fusion) | data formatting | bytes 1048576 | tf_op jit(solution)/shard_map/stw,pw->stp/dot_general | solution.py:61
  85.2 5.0 %convolution_bitcast_fusion = f32[4,16,256]{1,0,2:T(4,128)S(1)} fusion(f32[32,16,256]{0,1,2:T(8,128)} %copy.22, f32[32,4,256]{0,1,2:T(4,128)S(1)} %copy.23), kind=kOutput, calls=%fused_computation.5 | convolution fusion | flops 6291456 | bytes 720896 | tf_op jit(solution)/shard_map/srp,stp->rtp/dot_general | solution.py:62
  90.2 0.2 copy.24
  90.4 0.7 fusion.2
  (18 shorter events, 0.2 us)
Async XLA Ops:
  6.5 9.8 %copy-start = (bf16[16,16,4096]{2,1,0:T(8,128)(2,1)S(1)}, bf16[16,16,4096]{2,1,0:T(8,128)(2,1)}, u32[]{:S(2)}) copy-start(bf16[16,16,4096]{2,1,0:T(8,128)(2,1)} %param.9) | copy-start | bytes 6291460
  11.2 12.5 %all-to-all-start.1 = ((bf16[8,4,16]{2,1,0:T(4,128)(2,1)}), bf16[8,4,16]{2,1,0:T(4,128)(2,1)S(1)}, u32[]{:S(2)}, u32[]{:S(2)}) async-start(bf16[8,4,16]{2,1,0:T(4,128)(2,1)} %select_convert_fusion), calls=%async_computation.1 | async-start | bytes 16384 | tf_op jit(solution)/shard_map/all_to_all | solution.py:47
  23.7 5.5 %copy-start.1 = (f32[1200]{0:T(1024)S(1)}, f32[1200]{0:T(1024)}, u32[]{:S(2)}) copy-start(f32[1200]{0:T(1024)} %param.15) | copy-start | bytes 14404
  23.7 5.5 %copy-start.2 = (s32[256]{0:T(256)S(1)}, s32[256]{0:T(256)}, u32[]{:S(2)}) copy-start(s32[256]{0:T(256)} %param.16) | copy-start | bytes 3076
  23.7 5.5 %copy-start.3 = (s32[256]{0:T(256)S(1)}, s32[256]{0:T(256)}, u32[]{:S(2)}) copy-start(s32[256]{0:T(256)} %param.17) | copy-start | bytes 3076
  23.7 54.8 %all-to-all-start = ((bf16[32,16,4096]{2,1,0:T(8,128)(2,1)}), bf16[32,16,4096]{2,1,0:T(8,128)(2,1)}, u32[]{:S(2)}, u32[]{:S(2)}) async-start(bf16[32,16,4096]{2,1,0:T(8,128)(2,1)} %broadcast_select_fusion), calls=%async_computation | async-start | bytes 8388608 | tf_op jit(solution)/shard_map/all_to_all | solution.py:46
  28.4 50.1 %all-gather.2.cloned.1.call-start = ((), (), s32[]{:S(2)}) async-start(), calls=%async_computation.2 | async-start | bytes 2621440 | tf_op jit(solution)/shard_map/all_gather | solution.py:50
  85.2 5.2 %copy-start.4 = (f32[64]{0:T(128)S(1)}, f32[64]{0:T(128)}, u32[]{:S(2)}) copy-start(f32[64]{0:T(128)} %param.14) | copy-start | bytes 772
Sparse Core Ops, SparseCore 0:
  30.8 47.6 all-gather.1
where the time goes:
time: 98.4 us; the launch traced here: 97.9 us
  waiting for transfers between devices  49.1 us (50%)
  between operations  13.5 us (14%)
  starting transfers between devices  9.9 us (10%)
  other arithmetic  9.47 us (10%)
  matrix products  9.28 us (9%)
  local copies, waits for them, and re-layouts  6.7 us (7%)
    all_gather x1, waiting for transfers between devices, body(): panel = lax.all_gather(amplitudes, 'blk', axis=0, tiled=True)  48.4 us
    all_to_all x1, starting transfers between devices, body(): lax.all_to_all(sent_coef, 'virt', split_axis=0, concat_axis=0, tiled=True)  5.17 us
    dot_general x1, matrix products, body(): jnp.einsum('srp,stp->rtp', columns, product, precision=lax.Precision.HIGH...  4.99 us
    all_to_all x1, starting transfers between devices, body(): lax.all_to_all(sent_tiles, 'virt', split_axis=0, concat_axis=0, tiled=True)  4.69 us
    select_n x1, other arithmetic, body(): jnp.where(filled[:, None, None], integrals[source_tile], jnp.zeros((), jn...  4.5 us
    dot_general x1, matrix products, body(): jnp.einsum('stw,pw->stp', got_tiles, panel, preferred_element_type=jnp.fl...  4.15 us
    gather x1, local copies, waits for them, and re-layouts, body(): integrals[source_tile]  2.79 us
    dot_general x1, local copies, waits for them, and re-layouts, body(): jnp.einsum('stw,pw->stp', got_tiles, panel, preferred_element_type=jnp.fl...  2.62 us
  transfers between devices with their start and end apart: 3, of which 1 were waited for; matrix products, arithmetic and copies ran while one was open for 8% of the time, Pallas kernels for 0%

commit v1 on v0

--- a/solution.py
+++ b/solution.py
@@ -47,7 +47,20 @@
         lax.all_to_all(sent_coef, "virt", split_axis=0, concat_axis=0, tiled=True),
     )
     got_coef = got_coef.astype(jnp.float32).reshape(slot_count, row_blocks, blk_count)
-    panel = lax.all_gather(amplitudes, "blk", axis=0, tiled=True)
+    ways, here, step = (lax.axis_size("blk"), lax.axis_index("blk"), amplitudes.shape[0])
+    dims = [n * ways if d == 0 else n for d, n in enumerate(amplitudes.shape)]
+    panel = lax.dynamic_update_slice_in_dim(
+        jnp.zeros(dims, amplitudes.dtype), amplitudes, here * step, axis=0
+    )
+    going_up = going_down = amplitudes
+    for far in range(1, ways // 2 + 1):
+        going_up = lax.ppermute(going_up, "blk", [(d, (d + 1) % ways) for d in range(ways)])
+        panel = lax.dynamic_update_slice_in_dim(panel, going_up, (here - far) % ways * step, axis=0)
+        if 2 * far < ways:
+            going_down = lax.ppermute(going_down, "blk", [(d, (d - 1) % ways) for d in range(ways)])
+            panel = lax.dynamic_update_slice_in_dim(
+                panel, going_down, (here + far) % ways * step, axis=0
+            )
     column_count = panel.shape[0]
     column_panel = jnp.arange(column_count, dtype=jnp.int32) // panel_rows
     columns = jnp.einsum(

time: 98.4 us -> 84.1 us (0.85)
  between operations: 13.5 us -> 0.1 us
  waiting for transfers between devices: 49.1 us -> 37.2 us
  local copies, waits for them, and re-layouts: 6.7 us -> 13.9 us
  starting transfers between devices: 9.9 us -> 13.7 us
    all_gather x1 -> x0, waiting for transfers between devices: 48.4 us -> none  [body(): panel = lax.all_gather(amplitudes, 'blk', axis=0, tiled=True)]
    ppermute x0 -> x3, waiting for transfers between devices: none -> 27.6 us  [the longest x2 19.3 us: body(): lax.ppermute(going_up, 'blk', [(d, (d + 1) % ways) for d in range(ways)])]
    all_to_all x1, waiting for transfers between devices: 0.01 us -> 9.53 us  [body(): lax.all_to_all(sent_tiles, 'virt', split_axis=0, concat_axis=0, tiled=True)]
    dynamic_update_slice x0 -> x4, local copies, waits for them, and re-layouts: none -> 5.55 us  [the longest x2 2.73 us: body(): lax.dynamic_update_slice_in_dim(panel, going_up, (here - far) % ways * st...]
    ppermute x0 -> x3, starting transfers between devices: none -> 3.88 us  [the longest x1 2.25 us: body(): lax.ppermute(going_down, 'blk', [(d, (d - 1) % ways) for d in range(ways)])]
    broadcast_in_dim x0 -> x1, local copies, waits for them, and re-layouts: none -> 1.63 us  [body(): jnp.zeros(dims, amplitudes.dtype)]
  transfers between devices with their start and end apart: 3 -> 5, of which waited for: 1 -> 4; matrix products, arithmetic and copies ran while one was open for 8% -> 18% of each run, Pallas kernels for 0% -> 0%
where the time goes in v1:
time: 84.1 us; the launch traced here: 83.6 us
  waiting for transfers between devices  37.2 us (44%)
  local copies, waits for them, and re-layouts  13.9 us (17%)
  starting transfers between devices  13.7 us (16%)
  other arithmetic  9.47 us (11%)
  matrix products  9.28 us (11%)
    ppermute x2, waiting for transfers between devices, body(): lax.ppermute(going_up, 'blk', [(d, (d + 1) % ways) for d in range(ways)])  19.3 us
    all_to_all x1, waiting for transfers between devices, body(): lax.all_to_all(sent_tiles, 'virt', split_axis=0, concat_axis=0, tiled=True)  9.53 us
    ppermute x1, waiting for transfers between devices, body(): lax.ppermute(going_down, 'blk', [(d, (d - 1) % ways) for d in range(ways)])  8.37 us
    all_to_all x1, starting transfers between devices, body(): lax.all_to_all(sent_coef, 'virt', split_axis=0, concat_axis=0, tiled=True)  5.17 us
    dot_general x1, matrix products, body(): jnp.einsum('srp,stp->rtp', columns, product, precision=lax.Precision.HIGH...  4.99 us
    all_to_all x1, starting transfers between devices, body(): lax.all_to_all(sent_tiles, 'virt', split_axis=0, concat_axis=0, tiled=True)  4.68 us
    select_n x1, other arithmetic, body(): jnp.where(filled[:, None, None], integrals[source_tile], jnp.zeros((), jn...  4.5 us
    dot_general x1, matrix products, body(): jnp.einsum('stw,pw->stp', got_tiles, panel, preferred_element_type=jnp.fl...  4.15 us
  transfers between devices with their start and end apart: 5, of which 4 were waited for; matrix products, arithmetic and copies ran while one was open for 18% of the time, Pallas kernels for 0%

profile of v1, /device:TPU:0, one launch (start us, length us, event | category | flops | bytes accessed | tf_op | source)
XLA Modules:
  0.0 83.6 jit_solution(344246022727164185)
XLA Ops:
  0.0 1.0 %convert_reduce_fusion = s32[16]{0:T(128)S(1)} fusion(s32[16]{0:T(128)} %param.11), kind=kLoop, calls=%fused_computation.16 | loop fusion | flops 1264 | bytes 128 | tf_op jit(solution)/shard_map/reduce_sum | solution.py:29
  1.0 0.7 multiply_add_fusion
  1.9 0.7 convert_element_type.25
  2.6 0.7 fusion.10
  4.0 0.7 select_convert_fusion
  4.7 5.2 %all-to-all-start.1 = ((bf16[8,4,16]{2,1,0:T(4,128)(2,1)}), bf16[8,4,16]{2,1,0:T(4,128)(2,1)S(1)}, u32[]{:S(2)}, u32[]{:S(2)}) async-start(bf16[8,4,16]{2,1,0:T(4,128)(2,1)} %select_convert_fusion), calls=%async_computation.1 | async-start | bytes 16384 | tf_op jit(solution)/shard_map/all_to_all | solution.py:47
  9.8 2.8 %gather_fusion = bf16[32,16,4096]{2,1,0:T(8,128)(2,1)} fusion(bf16[16,16,4096]{2,1,0:T(8,128)(2,1)S(1)} %copy-done, s32[1024]{0:T(1024)S(1)} %pad_clamp_fusion), kind=kCustom, calls=%fused_computation | custom fusion | bytes 8388736 | tf_op jit(solution)/shard_map/gather | solution.py:39
  12.6 4.5 %broadcast_select_fusion = bf16[32,16,4096]{2,1,0:T(8,128)(2,1)} fusion(bf16[32,16,4096]{2,1,0:T(8,128)(2,1)} %gather_fusion, pred[32]{0:T(512)(128)(4,1)S(1)} %fusion.5), kind=kLoop, calls=%fused_computation.2 | loop fusion | flops 2097152 | bytes 8388640 | tf_op jit(solution)/shard_map/jit(_where)/select_n | solution.py:38
  17.1 4.7 %all-to-all-start = ((bf16[32,16,4096]{2,1,0:T(8,128)(2,1)}), bf16[32,16,4096]{2,1,0:T(8,128)(2,1)}, u32[]{:S(2)}, u32[]{:S(2)}) async-start(bf16[32,16,4096]{2,1,0:T(8,128)(2,1)} %broadcast_select_fusion), calls=%async_computation | async-start | bytes 8388608 | tf_op jit(solution)/shard_map/all_to_all | solution.py:46
  21.9 1.6 %collective-permute-start = (bf16[64,4096]{1,0:T(8,128)(2,1)S(1)}, bf16[64,4096]{1,0:T(8,128)(2,1)}, u32[]{:S(2)}, u32[]{:S(2)}) collective-permute-start(bf16[64,4096]{1,0:T(8,128)(2,1)S(1)} %copy-done.1), channel_id=1, source_target_pairs={{0,8},{8,16},{16,24},{24,0},{1,9},{9,17},{17,25},{25,1},{2,10},{10... | collective-permute-start | bytes 1572872 | tf_op jit(solution)/shard_map/ppermute | solution.py:57
  23.5 2.2 %collective-permute-start.1 = (bf16[64,4096]{1,0:T(8,128)(2,1)S(1)}, bf16[64,4096]{1,0:T(8,128)(2,1)}, u32[]{:S(2)}, u32[]{:S(2)}) collective-permute-start(bf16[64,4096]{1,0:T(8,128)(2,1)S(1)} %copy-done.1), channel_id=1, source_target_pairs={{0,24},{8,0},{16,8},{24,16},{1,25},{9,1},{17,9},{25,17},{2,26},{10... | collective-permute-start | bytes 1572872 | tf_op jit(solution)/shard_map/ppermute | solution.py:60
  25.7 1.6 %broadcast_in_dim.46 = bf16[256,4096]{1,0:T(8,128)(2,1)} broadcast(bf16[]{:T(256)} %constant.53.clone.1), dimensions={} | broadcast | bytes 2097154 | tf_op jit(solution)/shard_map/broadcast_in_dim | solution.py:53
  27.4 0.9 %constant_dynamic-update-slice_fusion.3 = bf16[256,4096]{1,0:T(8,128)(2,1)} fusion(bf16[256,4096]{1,0:T(8,128)(2,1)} %broadcast_in_dim.46, bf16[64,4096]{1,0:T(8,128)(2,1)S(1)} %copy-done.1, s32[]{:T(128)S(6)} %select_n.65), kind=kLoop, calls=%fused_computation.36 | loop fusion | bytes 1048580 | tf_op jit(solution)/shard_map/dynamic_update_slice | solution.py:52
  29.1 9.5 %collective-permute-done = bf16[64,4096]{1,0:T(8,128)(2,1)} collective-permute-done((bf16[64,4096]{1,0:T(8,128)(2,1)S(1)}, bf16[64,4096]{1,0:T(8,128)(2,1)}, u32[]{:S(2)}, u32[]{:S(2)}) %collective-permute-start) | collective-permute-done | bytes 524320 | tf_op jit(solution)/shard_map/ppermute | solution.py:57
  38.6 1.9 %constant_dynamic-update-slice_fusion.2 = bf16[256,4096]{1,0:T(8,128)(2,1)} fusion(bf16[256,4096]{1,0:T(8,128)(2,1)} %constant_dynamic-update-slice_fusion.3, bf16[64,4096]{1,0:T(8,128)(2,1)} %collective-permute-done, s32[]{:T(128)S(6)} %select_n.67), kind=kLoop, calls=%fused_computation.35 | loop fusion | bytes 1048580 | tf_op jit(solution)/shard_map/dynamic_update_slice | solution.py:58
  40.5 8.4 %collective-permute-done.1 = bf16[64,4096]{1,0:T(8,128)(2,1)} collective-permute-done((bf16[64,4096]{1,0:T(8,128)(2,1)S(1)}, bf16[64,4096]{1,0:T(8,128)(2,1)}, u32[]{:S(2)}, u32[]{:S(2)}) %collective-permute-start.1) | collective-permute-done | bytes 524320 | tf_op jit(solution)/shard_map/ppermute | solution.py:60
  48.9 1.9 %constant_dynamic-update-slice_fusion.1 = bf16[256,4096]{1,0:T(8,128)(2,1)} fusion(bf16[256,4096]{1,0:T(8,128)(2,1)} %constant_dynamic-update-slice_fusion.2, bf16[64,4096]{1,0:T(8,128)(2,1)} %collective-permute-done.1, s32[]{:T(128)S(6)} %select_n.69), kind=kLoop, calls=%fused_computation.34 | loop fusion | bytes 1048580 | tf_op jit(solution)/shard_map/dynamic_update_slice | solution.py:61
  50.8 9.8 %collective-permute-done.2 = bf16[64,4096]{1,0:T(8,128)(2,1)S(1)} collective-permute-done((bf16[64,4096]{1,0:T(8,128)(2,1)}, bf16[64,4096]{1,0:T(8,128)(2,1)S(1)}, u32[]{:S(2)}, u32[]{:S(2)}) %collective-permute-start.2) | collective-permute-done | bytes 524320 | tf_op jit(solution)/shard_map/ppermute | solution.py:57
  60.6 0.8 constant_dynamic-update-slice_fusion
  61.4 9.5 %all-to-all-done = bf16[32,16,4096]{2,1,0:T(8,128)(2,1)} async-done(((bf16[32,16,4096]{2,1,0:T(8,128)(2,1)}), bf16[32,16,4096]{2,1,0:T(8,128)(2,1)}, u32[]{:S(2)}, u32[]{:S(2)}) %all-to-all-start) | async-done | bytes 4194336 | tf_op jit(solution)/shard_map/all_to_all | solution.py:46
  71.0 4.1 %fusion = f32[32,16,256]{2,1,0:T(8,128)S(1)} fusion(bf16[32,16,4096]{2,1,0:T(8,128)(2,1)} %all-to-all-done, bf16[256,4096]{1,0:T(8,128)(2,1)} %constant_dynamic-update-slice_fusion), kind=kOutput, calls=%fused_computation.3 | convolution fusion | flops 1073741824 | bytes 6815744 | tf_op jit(solution)/shard_map/stw,pw->stp/dot_general | solution.py:74
  75.1 2.6 %copy.22 = f32[32,16,256]{0,1,2:T(8,128)} copy(f32[32,16,256]{2,1,0:T(8,128)S(1)} %fusion) | data formatting | bytes 1048576 | tf_op jit(solution)/shard_map/stw,pw->stp/dot_general | solution.py:74
  77.7 5.0 %convolution_bitcast_fusion = f32[4,16,256]{1,0,2:T(4,128)S(1)} fusion(f32[32,16,256]{0,1,2:T(8,128)} %copy.22, f32[32,4,256]{0,1,2:T(4,128)S(1)} %copy.23), kind=kOutput, calls=%fused_computation.5 | convolution fusion | flops 6291456 | bytes 720896 | tf_op jit(solution)/shard_map/srp,stp->rtp/dot_general | solution.py:75
  82.9 0.7 fusion.2
  (28 shorter events, 2.0 us)
Async XLA Ops:
  0.0 9.8 %copy-start = (bf16[16,16,4096]{2,1,0:T(8,128)(2,1)S(1)}, bf16[16,16,4096]{2,1,0:T(8,128)(2,1)}, u32[]{:S(2)}) copy-start(bf16[16,16,4096]{2,1,0:T(8,128)(2,1)} %param.9) | copy-start | bytes 6291460
  4.7 12.5 %all-to-all-start.1 = ((bf16[8,4,16]{2,1,0:T(4,128)(2,1)}), bf16[8,4,16]{2,1,0:T(4,128)(2,1)S(1)}, u32[]{:S(2)}, u32[]{:S(2)}) async-start(bf16[8,4,16]{2,1,0:T(4,128)(2,1)} %select_convert_fusion), calls=%async_computation.1 | async-start | bytes 16384 | tf_op jit(solution)/shard_map/all_to_all | solution.py:47
  17.1 4.7 %copy-start.1 = (bf16[64,4096]{1,0:T(8,128)(2,1)S(1)}, bf16[64,4096]{1,0:T(8,128)(2,1)}, u32[]{:S(2)}) copy-start(bf16[64,4096]{1,0:T(8,128)(2,1)} %param.10) | copy-start | bytes 1572868
  17.1 53.8 %all-to-all-start = ((bf16[32,16,4096]{2,1,0:T(8,128)(2,1)}), bf16[32,16,4096]{2,1,0:T(8,128)(2,1)}, u32[]{:S(2)}, u32[]{:S(2)}) async-start(bf16[32,16,4096]{2,1,0:T(8,128)(2,1)} %broadcast_select_fusion), calls=%async_computation | async-start | bytes 8388608 | tf_op jit(solution)/shard_map/all_to_all | solution.py:46
  21.8 6.4 %copy-start.2 = (f32[1200]{0:T(1024)S(1)}, f32[1200]{0:T(1024)}, u32[]{:S(2)}) copy-start(f32[1200]{0:T(1024)} %param.15) | copy-start | bytes 14404
  21.8 6.4 %copy-start.3 = (s32[256]{0:T(256)S(1)}, s32[256]{0:T(256)}, u32[]{:S(2)}) copy-start(s32[256]{0:T(256)} %param.16) | copy-start | bytes 3076
  21.9 6.4 %copy-start.4 = (s32[256]{0:T(256)S(1)}, s32[256]{0:T(256)}, u32[]{:S(2)}) copy-start(s32[256]{0:T(256)} %param.17) | copy-start | bytes 3076
  21.9 16.7 %collective-permute-start = (bf16[64,4096]{1,0:T(8,128)(2,1)S(1)}, bf16[64,4096]{1,0:T(8,128)(2,1)}, u32[]{:S(2)}, u32[]{:S(2)}) collective-permute-start(bf16[64,4096]{1,0:T(8,128)(2,1)S(1)} %copy-done.1), channel_id=1, source_target_pairs={{0,8},{8,16},{16,24},{24,0},{1,9},{9,17},{17,25},{25,1},{2,10},{10... | collective-permute-start | bytes 1572872 | tf_op jit(solution)/shard_map/ppermute | solution.py:57
  23.5 25.4 %collective-permute-start.1 = (bf16[64,4096]{1,0:T(8,128)(2,1)S(1)}, bf16[64,4096]{1,0:T(8,128)(2,1)}, u32[]{:S(2)}, u32[]{:S(2)}) collective-permute-start(bf16[64,4096]{1,0:T(8,128)(2,1)S(1)} %copy-done.1), channel_id=1, source_target_pairs={{0,24},{8,0},{16,8},{24,16},{1,25},{9,1},{17,9},{25,17},{2,26},{10... | collective-permute-start | bytes 1572872 | tf_op jit(solution)/shard_map/ppermute | solution.py:60
  38.6 22.0 %collective-permute-start.2 = (bf16[64,4096]{1,0:T(8,128)(2,1)}, bf16[64,4096]{1,0:T(8,128)(2,1)S(1)}, u32[]{:S(2)}, u32[]{:S(2)}) collective-permute-start(bf16[64,4096]{1,0:T(8,128)(2,1)} %collective-permute-done), channel_id=1, source_target_pairs={{0,8},{8,16},{16,24},{24,0},{1,9},{9,17},{17,25},{25,1},{2,10},{10... | collective-permute-start | bytes 1572872 | tf_op jit(solution)/shard_map/ppermute | solution.py:57
  77.7 5.2 %copy-start.5 = (f32[64]{0:T(128)S(1)}, f32[64]{0:T(128)}, u32[]{:S(2)}) copy-start(f32[64]{0:T(128)} %param.14) | copy-start | bytes 772
